TPU v7x, 32 devices: a whole 2x2x4 slice. The times are simulated.
32 devices in a mesh: row: 4 (over z), col: 8 (over y, x, core).
Axes of the slice: x: 2, y: 2, z: 4, core: 2. Of those that a mesh axis runs over, the one named last changes fastest.
Arguments:
- positions: float32 [3, 65536], P(None, ('row', 'col')), may hold values from 0 to 1
- masses: float32 [1, 65536], P(None, ('row', 'col')), may hold values from 2e-09 to 2e-08
- counts: int32 [1, 512], P(None, ('row', 'col')), may hold values from 32 to 128
- sources: int32 [512, 8], P(('row', 'col')), may hold values from 0 to 47, as said below
Outputs:
- accel: float32 [3, 65536], P(None, ('row', 'col'))
Inputs may be any that keep to these rules, and one draw needn't show every extreme that they name: `sources`: each device's source ids name exactly 4 distinct leaves of the lower row neighbour and exactly 4 of the upper one.
All inputs are finite; a program needn't handle non-finite values.
Results may differ from a plain program's by a relative error of at most 0.00024.
Values sent between devices are 32-bit elements; how exact they have to be, the bound alone decides.
A program may use at most 64 MiB of HBM per device.

v0:
```python
import jax
import jax.numpy as jnp
from jax import lax
from jax.sharding import PartitionSpec as P

softening = 2.5e-07


def padded_2(shard, sides, width):
    for axis, dim in sides:
        size, length = (lax.axis_size(axis), shard.shape[dim])
        up = [(i, (i + 1) % size) for i in range(size)]
        down = [(j, i) for i, j in up]
        last = lax.slice_in_dim(shard, length - width, length, axis=dim)
        leading = lax.slice_in_dim(shard, 0, width, axis=dim)
        before = lax.ppermute(last, axis, up)
        after = lax.ppermute(leading, axis, down)
        shard = jnp.concatenate([before, shard, after], axis=dim)
    return shard


def leaf_forces(full_table, targets, sources, alive):
    count = targets.shape[0]
    width = targets.shape[2]
    target_groups = targets.reshape(count // 8, 8, 4, width)
    source_groups = sources.reshape(count // 8, 8, sources.shape[1])
    alive_groups = alive.reshape(count // 8, 8, width)

    def one_group(items):
        target, index, living = items
        source = full_table[index]
        delta_x = source[:, :, 0, None, :] - target[:, None, 0, :, None]
        delta_y = source[:, :, 1, None, :] - target[:, None, 1, :, None]
        delta_z = source[:, :, 2, None, :] - target[:, None, 2, :, None]
        spread = softening + delta_x * delta_x + delta_y * delta_y + delta_z * delta_z
        weight = source[:, :, 3, None, :] / (spread * jnp.sqrt(spread))
        pull_x = jnp.sum(weight * delta_x, axis=(1, 3))
        pull_y = jnp.sum(weight * delta_y, axis=(1, 3))
        pull_z = jnp.sum(weight * delta_z, axis=(1, 3))
        return jnp.stack([pull_x, pull_y, pull_z], axis=1) * living[:, None, :]

    out = lax.map(one_group, (target_groups, source_groups, alive_groups))
    return out.reshape(count, 3, width)


def on_device(positions, masses, counts, sources):
    coords, weights, livecount = (
        lax.all_to_all(positions, "col", split_axis=1, concat_axis=1, tiled=True),
        lax.all_to_all(masses, "col", split_axis=1, concat_axis=1, tiled=True),
        lax.all_to_all(counts, "col", split_axis=1, concat_axis=1, tiled=True),
    )
    leaves = livecount.shape[1]
    width = coords.shape[1] // leaves
    alive = (
        lax.broadcasted_iota(jnp.int32, (leaves, width), 1) < livecount.reshape(leaves, 1)
    ).astype(jnp.float32)
    table = jnp.concatenate(
        [coords.reshape(3, leaves, width), (weights.reshape(leaves, width) * alive)[None]], axis=0
    )
    table = table.transpose(1, 0, 2)
    padded = padded_2(table, (("row", 0),), leaves)
    full = jnp.concatenate(
        [padded[leaves : 2 * leaves], padded[:leaves], padded[2 * leaves :]], axis=0
    )
    result = leaf_forces(full, table, sources, alive)
    return result.transpose(1, 0, 2).reshape(3, leaves * width)


def solution(mesh):
    return jax.shard_map(
        on_device,
        mesh=mesh,
        in_specs=(
            P(None, ("row", "col")),
            P(None, ("row", "col")),
            P(None, ("row", "col")),
            P(("row", "col"), None),
        ),
        out_specs=P(None, ("row", "col")),
        check_vma=False,
    )
```

profile of v0, /device:TPU:0, one launch (start us, length us, event | category | flops | bytes accessed | tf_op | source)
XLA Modules:
  0.0 44.4 jit_solution(10030716377979728203)
XLA Ops:
  0.0 0.6 %broadcast.80 = s32[]{:T(128)} broadcast(s32[]{:T(128)} %copy.43), dimensions={} | broadcast | bytes 8 | tf_op args[2]
  0.6 1.4 %reduce.8 = s32[16]{0:T(128)S(1)} reduce(s32[1,16]{1,0:T(1,128)} %param.8, s32[]{:T(128)} %broadcast.80), dimensions={0}, to_apply=%param.8.reduce_sub_computation.3 | reduce | bytes 132 | tf_op args[2]
  2.0 0.1 all_to_all.20
  2.0 9.7 %all_to_all.27 = s32[1,8,2]{2,0,1:T(1,128)S(1)} all-to-all(s32[1,8,2]{2,0,1:T(1,128)S(1)} %bitcast.86), channel_id=1, replica_groups=mesh['row'=4,'col'=8] {'col'}, dimensions={1} | all-to-all | bytes 128 | tf_op jit(solution)/shard_map/all_to_all | solution.py:50
  11.7 3.3 %all-to-all-start.2 = ((f32[1,8,256]{2,0,1:T(1,128)}), f32[1,8,256]{2,0,1:T(1,128)S(1)}, u32[]{:S(2)}, u32[]{:S(2)}) async-start(f32[1,8,256]{2,0,1:T(1,128)} %bitcast.87), calls=%async_computation.2 | async-start | bytes 16384 | tf_op jit(solution)/shard_map/all_to_all | solution.py:49
  15.1 0.8 %copy.28 = s32[16,8]{1,0:T(8,128)S(1)} copy(s32[16,8]{0,1:T(8,128)} %param.9) | data formatting | bytes 1024 | tf_op jit(solution)/shard_map/while | solution.py:42
  15.8 0.7 %reduce.9 = s32[8,2]{1,0:T(8,128)S(1)} reduce(s32[1,8,2]{2,0,1:T(1,128)S(1)} %all_to_all.27, s32[]{:T(128)} %broadcast.80), dimensions={0}, to_apply=%all_to_all.21.reduce_sub_computation.5 | reduce | bytes 132 | tf_op jit(solution)/shard_map/all_to_all | solution.py:50
  16.5 0.1 lt.37
  16.7 3.0 %all-to-all-done.2 = f32[1,8,256]{2,0,1:T(1,128)S(1)} async-done(((f32[1,8,256]{2,0,1:T(1,128)}), f32[1,8,256]{2,0,1:T(1,128)S(1)}, u32[]{:S(2)}, u32[]{:S(2)}) %all-to-all-start.2) | async-done | bytes 8224 | tf_op jit(solution)/shard_map/all_to_all | solution.py:49
  19.7 3.3 %all-to-all-start = ((f32[3,8,256]{2,0,1:T(4,128)}), f32[3,8,256]{2,0,1:T(4,128)S(1)}, u32[]{:S(2)}, u32[]{:S(2)}) async-start(f32[3,8,256]{2,0,1:T(4,128)} %bitcast.83), calls=%async_computation | async-start | bytes 65536 | tf_op jit(solution)/shard_map/all_to_all | solution.py:48
  23.1 4.7 %all-to-all-done = f32[3,8,256]{2,0,1:T(4,128)S(1)} async-done(((f32[3,8,256]{2,0,1:T(4,128)}), f32[3,8,256]{2,0,1:T(4,128)S(1)}, u32[]{:S(2)}, u32[]{:S(2)}) %all-to-all-start) | async-done | bytes 24608 | tf_op jit(solution)/shard_map/all_to_all | solution.py:48
  27.8 1.6 %collective-permute-start = (f32[16,4,128]{2,0,1:T(8,128)S(1)}, f32[16,4,128]{2,0,1:T(8,128)S(1)}, u32[]{:S(2)}, u32[]{:S(2)}) collective-permute-start(f32[16,4,128]{2,0,1:T(8,128)S(1)} %get-tuple-element.91), channel_id=1, source_target_pairs={{0,8},{8,16},{16,24},{24,0},{1,9},{9,17},{17,25},{25,1},{2,10},{10... | collective-permute-start | bytes 98312 | tf_op jit(solution)/shard_map/ppermute | solution.py:16
  29.5 2.2 %collective-permute-start.1 = (f32[16,4,128]{2,0,1:T(8,128)S(1)}, f32[16,4,128]{2,0,1:T(8,128)S(1)}, u32[]{:S(2)}, u32[]{:S(2)}) collective-permute-start(f32[16,4,128]{2,0,1:T(8,128)S(1)} %get-tuple-element.91), channel_id=1, source_target_pairs={{8,0},{16,8},{24,16},{0,24},{9,1},{17,9},{25,17},{1,25},{10,2},{18... | collective-permute-start | bytes 98312 | tf_op jit(solution)/shard_map/ppermute | solution.py:17
  31.8 1.9 %collective-permute-done = f32[16,4,128]{2,0,1:T(8,128)S(1)} collective-permute-done((f32[16,4,128]{2,0,1:T(8,128)S(1)}, f32[16,4,128]{2,0,1:T(8,128)S(1)}, u32[]{:S(2)}, u32[]{:S(2)}) %collective-permute-start) | collective-permute-done | bytes 32800 | tf_op jit(solution)/shard_map/ppermute | solution.py:16
  33.8 10.0 %while.10 = (s32[]{:T(128)}, f32[2,8,3,128]{3,1,0,2:T(8,128)S(1)}, s32[2,8,8]{2,1,0:T(8,128)S(1)}, f32[48,4,128]{2,1,0:T(4,128)S(1)}, f32[2,8,4,128]{3,1,0,2:T(8,128)S(1)}, /*index=5*/f32[2,8,128]{2,1,0:T(8,128)S(1)}, s32[]{:T(128)}) while((s32[]{:T(128)}, f32[2,8,3,128]{3,1,0,2:T(8,128)S(1)}, s32[2,8,8]{2,1,0:T(8,128)S(1)}, ...), condition=%wide.region_4.5_spmd, body=%wide.region_0.4_spmd.sunk | while | flops 17833152 | bytes 779869 | solution.py:42
  33.8 0.1 reshape.198
  33.9 0.7 %gather_fusion = f32[64,4,128]{2,1,0:T(4,128)S(1)} fusion(f32[48,4,128]{2,1,0:T(4,128)S(1)} %get-tuple-element.166, s32[1024]{0:T(1024)S(1)} %pad_clamp_fusion.2), kind=kCustom, calls=%fused_computation.clone.1 | custom fusion | bytes 262400 | tf_op jit(solution)/shard_map/while/body/eval_jaxpr/gather | solution.py:31
  34.6 0.1 fusion.17
  34.7 4.0 %fusion.18 = (f32[8,128]{1,0:T(8,128)S(1)}, f32[8,128]{1,0:T(8,128)S(1)}, f32[8,128]{1,0:T(8,128)S(1)}) fusion(f32[8,128]{1,0:T(8,128)S(1)} %get-tuple-element.139, f32[8,8,128]{2,1,0:T(8,128)S(1)} %bitcast.76, f32[8,128]{1,0:T(8,128)S(1)} %get-tuple-element.141, f32[8,8,128]{2,1,0:T(8,128)S(1)} %bitcast.77, f32[8,128]{1,0:T(8,128)S(1)} %get-tuple-element.143, ...), kind=kLoop, calls=%fused_computation.11.clone.1 | loop fusion | flops 17822720 | bytes 155648 | tf_op jit(solution)/shard_map/while/body/eval_jaxpr/reduce_sum | solution.py:37
  38.8 0.1 reshape.198
  38.9 0.7 %gather_fusion = f32[64,4,128]{2,1,0:T(4,128)S(1)} fusion(f32[48,4,128]{2,1,0:T(4,128)S(1)} %get-tuple-element.166, s32[1024]{0:T(1024)S(1)} %pad_clamp_fusion.2), kind=kCustom, calls=%fused_computation.clone.1 | custom fusion | bytes 262400 | tf_op jit(solution)/shard_map/while/body/eval_jaxpr/gather | solution.py:31
  39.6 0.1 fusion.17
  39.7 4.0 %fusion.18 = (f32[8,128]{1,0:T(8,128)S(1)}, f32[8,128]{1,0:T(8,128)S(1)}, f32[8,128]{1,0:T(8,128)S(1)}) fusion(f32[8,128]{1,0:T(8,128)S(1)} %get-tuple-element.139, f32[8,8,128]{2,1,0:T(8,128)S(1)} %bitcast.76, f32[8,128]{1,0:T(8,128)S(1)} %get-tuple-element.141, f32[8,8,128]{2,1,0:T(8,128)S(1)} %bitcast.77, f32[8,128]{1,0:T(8,128)S(1)} %get-tuple-element.143, ...), kind=kLoop, calls=%fused_computation.11.clone.1 | loop fusion | flops 17822720 | bytes 155648 | tf_op jit(solution)/shard_map/while/body/eval_jaxpr/reduce_sum | solution.py:37
  43.8 0.6 %copy.34 = f32[1,3,16,128]{3,1,2,0:T(4,128)} copy(f32[1,3,16,128]{3,2,1,0:T(8,128)S(1)} %bitcast.85) | data formatting | bytes 49152
  (22 shorter events, 0.4 us)
Async XLA Ops:
  11.7 8.0 %all-to-all-start.2 = ((f32[1,8,256]{2,0,1:T(1,128)}), f32[1,8,256]{2,0,1:T(1,128)S(1)}, u32[]{:S(2)}, u32[]{:S(2)}) async-start(f32[1,8,256]{2,0,1:T(1,128)} %bitcast.87), calls=%async_computation.2 | async-start | bytes 16384 | tf_op jit(solution)/shard_map/all_to_all | solution.py:49
  19.7 8.1 %all-to-all-start = ((f32[3,8,256]{2,0,1:T(4,128)}), f32[3,8,256]{2,0,1:T(4,128)S(1)}, u32[]{:S(2)}, u32[]{:S(2)}) async-start(f32[3,8,256]{2,0,1:T(4,128)} %bitcast.83), calls=%async_computation | async-start | bytes 65536 | tf_op jit(solution)/shard_map/all_to_all | solution.py:48
  27.8 5.9 %collective-permute-start = (f32[16,4,128]{2,0,1:T(8,128)S(1)}, f32[16,4,128]{2,0,1:T(8,128)S(1)}, u32[]{:S(2)}, u32[]{:S(2)}) collective-permute-start(f32[16,4,128]{2,0,1:T(8,128)S(1)} %get-tuple-element.91), channel_id=1, source_target_pairs={{0,8},{8,16},{16,24},{24,0},{1,9},{9,17},{17,25},{25,1},{2,10},{10... | collective-permute-start | bytes 98312 | tf_op jit(solution)/shard_map/ppermute | solution.py:16
  29.5 4.3 %collective-permute-start.1 = (f32[16,4,128]{2,0,1:T(8,128)S(1)}, f32[16,4,128]{2,0,1:T(8,128)S(1)}, u32[]{:S(2)}, u32[]{:S(2)}) collective-permute-start(f32[16,4,128]{2,0,1:T(8,128)S(1)} %get-tuple-element.91), channel_id=1, source_target_pairs={{8,0},{16,8},{24,16},{0,24},{9,1},{17,9},{25,17},{1,25},{10,2},{18... | collective-permute-start | bytes 98312 | tf_op jit(solution)/shard_map/ppermute | solution.py:17
where the time goes:
time: 44.8 us; the launch traced here: 44.4 us
  starting transfers between devices  10.6 us (24%)
  other arithmetic  10.4 us (23%)
  blocking collectives  9.68 us (22%)
  waiting for transfers between devices  9.65 us (22%)
  local copies, waits for them, and re-layouts  3.98 us (9%)
    all_to_all x1, blocking collectives, on_device(): lax.all_to_all(counts, 'col', split_axis=1, concat_axis=1, tiled=True)  9.68 us
    reduce_sum x2, other arithmetic, one_group(): pull_x = jnp.sum(weight * delta_x, axis=(1, 3))  8.08 us
    all_to_all x1, waiting for transfers between devices, on_device(): lax.all_to_all(positions, 'col', split_axis=1, concat_axis=1, tiled=True)  4.7 us
    all_to_all x1, starting transfers between devices, on_device(): lax.all_to_all(positions, 'col', split_axis=1, concat_axis=1, tiled=True)  3.34 us
    all_to_all x1, starting transfers between devices, on_device(): lax.all_to_all(masses, 'col', split_axis=1, concat_axis=1, tiled=True)  3.33 us
    all_to_all x1, waiting for transfers between devices, on_device(): lax.all_to_all(masses, 'col', split_axis=1, concat_axis=1, tiled=True)  3 us
    ppermute x1, starting transfers between devices, padded_2(): after = lax.ppermute(leading, axis, down)  2.25 us
    ppermute x1, waiting for transfers between devices, padded_2(): before = lax.ppermute(last, axis, up)  1.92 us
  transfers between devices with their start and end apart: 4, of which 3 were waited for; matrix products, arithmetic and copies ran while one was open for 4% of the time, Pallas kernels for 0%

commit v1 on v0

v1 whole, which is shorter than its diff:
```python
import functools

import jax
import jax.numpy as jnp
from jax import lax
from jax.experimental import pallas as pl
from jax.experimental.pallas import tpu as pltpu
from jax.sharding import PartitionSpec as P

softening = 2.5e-07
COMPONENTS = 4
CHUNK = 32
GROUP = 16
MESH = pl.DeviceIdType.MESH


def exchange_kernel(
    rows, cols, pos_hbm, mass_hbm, counts_hbm, table,
    pos, mass, counts, packed, in_sems, own_sem, send, recv, up_send, down_send, low_recv, high_recv,
):
    r, c = lax.axis_index("row"), lax.axis_index("col")
    up, down = lax.rem(r + 1, rows), lax.rem(r + rows - 1, rows)
    loads = [
        pltpu.make_async_copy(src, dst, in_sems.at[i])
        for i, (src, dst) in enumerate(((pos_hbm, pos), (mass_hbm, mass), (counts_hbm, counts)))
    ]
    for load in loads:
        load.start()

    barrier = pltpu.get_barrier_semaphore()
    pl.semaphore_signal(barrier, inc=1, device_id=(up, c), device_id_type=MESH)
    pl.semaphore_signal(barrier, inc=1, device_id=(down, c), device_id_type=MESH)

    def greet(o, carry):
        peer = lax.rem(c + o, cols)
        pl.semaphore_signal(barrier, inc=1, device_id=(r, peer), device_id_type=MESH)
        return carry

    lax.fori_loop(1, cols, greet, 0)
    for load in loads:
        load.wait()

    tile = packed.shape[1]
    blk = tile // COMPONENTS
    width = packed.shape[2]
    lane = lax.broadcasted_iota(jnp.int32, (1, width), 1)

    def pack(p, carry):
        for b in range(blk):
            leaf = p * blk + b
            here = pl.ds(pl.multiple_of(leaf * width, width), width)
            packed[p, COMPONENTS * b : COMPONENTS * b + 3, :] = pos[:, here]
            packed[p, COMPONENTS * b + 3 : COMPONENTS * b + 4, :] = jnp.where(
                lane < counts[0, leaf], mass[:, here], 0.0
            )
        return carry

    lax.fori_loop(0, cols, pack, 0, unroll=cols <= 8)
    pl.semaphore_wait(barrier, cols + 1)

    def across(o):
        peer = lax.rem(c + o, cols)
        return pltpu.make_async_remote_copy(
            src_ref=packed.at[peer], dst_ref=table.at[0, c],
            send_sem=send.at[peer], recv_sem=recv.at[c],
            device_id=(r, peer), device_id_type=MESH,
        )

    def along(src, p, to_up):
        return pltpu.make_async_remote_copy(
            src_ref=src, dst_ref=table.at[1 if to_up else 2, p],
            send_sem=(up_send if to_up else down_send).at[p],
            recv_sem=(low_recv if to_up else high_recv).at[p],
            device_id=(up if to_up else down, c), device_id_type=MESH,
        )

    def send_across(o, carry):
        across(o).start()
        return carry

    lax.fori_loop(1, cols, send_across, 0)
    along(packed.at[c], c, True).start()
    along(packed.at[c], c, False).start()
    own = pltpu.make_async_copy(packed.at[c], table.at[0, c], own_sem)
    own.start()

    def forward(o, carry):
        p = lax.bitwise_xor(c, o) if cols & (cols - 1) == 0 else lax.rem(c + o, cols)
        pltpu.make_async_remote_copy(
            src_ref=packed.at[p], dst_ref=table.at[0, p],
            send_sem=send.at[p], recv_sem=recv.at[p],
            device_id=(r, p), device_id_type=MESH,
        ).wait_recv()
        along(table.at[0, p], p, True).start()
        along(table.at[0, p], p, False).start()
        return carry

    lax.fori_loop(1, cols, forward, 0)
    own.wait()

    def settle_sends(o, carry):
        across(o).wait_send()
        return carry

    lax.fori_loop(1, cols, settle_sends, 0)

    def settle(p, carry):
        for to_up in (True, False):
            copy = along(table.at[0, p], p, to_up)
            copy.wait_send()
            copy.wait_recv()
        return carry

    lax.fori_loop(0, cols, settle, 0)


def exchange(rows, cols, positions, masses, counts):
    leaves = counts.shape[1]
    width = positions.shape[1] // leaves
    tile = COMPONENTS * (leaves // cols)
    dma = pltpu.SemaphoreType.DMA
    return pl.pallas_call(
        functools.partial(exchange_kernel, rows, cols),
        out_shape=jax.ShapeDtypeStruct((3, cols, tile, width), jnp.float32),
        in_specs=[pl.BlockSpec(memory_space=pl.ANY)] * 3,
        out_specs=pl.BlockSpec(memory_space=pltpu.VMEM),
        scratch_shapes=[
            pltpu.VMEM(positions.shape, jnp.float32),
            pltpu.VMEM(masses.shape, jnp.float32),
            pltpu.SMEM(counts.shape, jnp.int32),
            pltpu.VMEM((cols, tile, width), jnp.float32),
            dma((3,)), dma(()), dma((cols,)), dma((cols,)),
            dma((cols,)), dma((cols,)), dma((cols,)), dma((cols,)),
        ],
        compiler_params=pltpu.CompilerParams(collective_id=0, has_side_effects=True),
        name="exchange",
    )(positions, masses, counts)


def force_kernel(sources, table, out, spread_targets, pulls, live):
    width = table.shape[1]
    group = spread_targets.shape[0]
    per_list = sources.shape[1]
    ones = jnp.ones((8, width), jnp.float32)

    def one_group(g, carry):
        def prepare(i, carry):
            row = (g * group + i) * COMPONENTS
            for axis in range(3):
                line = table[pl.ds(row + axis, 1), :]
                spread_targets[i, axis] = jnp.broadcast_to(line, (width, width)).T
            alive = table[pl.ds(row + 3, 1), :] > 0.0
            live[i] = jnp.sum(alive.astype(jnp.int32))
            return carry

        lax.fori_loop(0, group, prepare, 0, unroll=4)

        def one_target(i, carry):
            ids = [sources[g * group + i, k] * COMPONENTS for k in range(per_list)]

            def one_chunk(n, carry):
                here = pl.ds(pl.multiple_of(n * CHUNK, CHUNK), CHUNK)
                tx, ty, tz = (spread_targets[i, axis, here, :] for axis in range(3))
                ax = ay = az = jnp.zeros((CHUNK, width), jnp.float32)
                for k in range(per_list):
                    dx = table[pl.ds(ids[k], 1), :] - tx
                    dy = table[pl.ds(ids[k] + 1, 1), :] - ty
                    dz = table[pl.ds(ids[k] + 2, 1), :] - tz
                    inverse = lax.rsqrt(softening + dx * dx + dy * dy + dz * dz)
                    weight = table[pl.ds(ids[k] + 3, 1), :] * inverse * (inverse * inverse)
                    ax, ay, az = ax + weight * dx, ay + weight * dy, az + weight * dz
                pulls[i, 0, here, :] = ax
                pulls[i, 1, here, :] = ay
                pulls[i, 2, here, :] = az
                return carry

            chunks = lax.div(live[i] + (CHUNK - 1), CHUNK)
            return lax.fori_loop(0, chunks, one_chunk, carry)

        lax.fori_loop(0, group, one_target, 0)

        def reduce(i, carry):
            t = g * group + i
            alive = table[pl.ds(t * COMPONENTS + 3, 1), :] > 0.0
            for axis in range(3):
                total = lax.dot_general(
                    ones, pulls[i, axis], (((1,), (1,)), ((), ())),
                    precision=lax.Precision.HIGHEST, preferred_element_type=jnp.float32,
                )
                out[axis : axis + 1, pl.ds(pl.multiple_of(t * width, width), width)] = jnp.where(
                    alive, total[0:1], 0.0
                )
            return carry

        lax.fori_loop(0, group, reduce, 0, unroll=4)
        return carry

    lax.fori_loop(0, sources.shape[0] // group, one_group, 0)


def forces(table, sources):
    leaves, width = sources.shape[0], table.shape[1]
    group = GROUP if leaves % GROUP == 0 else leaves
    return pl.pallas_call(
        force_kernel,
        out_shape=jax.ShapeDtypeStruct((3, leaves * width), jnp.float32),
        in_specs=[pl.BlockSpec(memory_space=pltpu.SMEM), pl.BlockSpec(memory_space=pltpu.VMEM)],
        out_specs=pl.BlockSpec(memory_space=pltpu.VMEM),
        scratch_shapes=[
            pltpu.VMEM((group, 3, width, width), jnp.float32),
            pltpu.VMEM((group, 3, width, width), jnp.float32),
            pltpu.SMEM((group,), jnp.int32),
        ],
        name="forces",
    )(sources, table)


def solution(mesh):
    rows, cols = mesh.shape["row"], mesh.shape["col"]

    def on_device(positions, masses, counts, sources):
        table = exchange(rows, cols, positions, masses, counts)
        return forces(table.reshape(-1, table.shape[-1]), sources)

    return jax.shard_map(
        on_device,
        mesh=mesh,
        in_specs=(
            P(None, ("row", "col")),
            P(None, ("row", "col")),
            P(None, ("row", "col")),
            P(("row", "col"), None),
        ),
        out_specs=P(None, ("row", "col")),
        check_vma=False,
    )
```

time: 44.8 us -> 27.1 us (0.60)
  Pallas kernels: 0 us -> 25.5 us
  starting transfers between devices: 10.6 us -> 0 us
  other arithmetic: 10.4 us -> 0 us
  blocking collectives: 9.68 us -> 0 us
  waiting for transfers between devices: 9.65 us -> 0 us
  local copies, waits for them, and re-layouts: 3.98 us -> 1.35 us
    pallas_call x0 -> x2, Pallas kernels: none -> 25.5 us  [the longest x1 12.9 us: exchange(): pl.pallas_call(functools.partial(exchange_kernel, rows, cols), out_shape=...]
    all_to_all x1 -> x0, blocking collectives: 9.68 us -> none  [on_device(): lax.all_to_all(counts, 'col', split_axis=1, concat_axis=1, tiled=True)]
    reduce_sum x2 -> x0, other arithmetic: 8.08 us -> none  [one_group(): pull_x = jnp.sum(weight * delta_x, axis=(1, 3))]
    all_to_all x2 -> x0, waiting for transfers between devices: 7.7 us -> none  [the longest x1 4.7 us: on_device(): lax.all_to_all(positions, 'col', split_axis=1, concat_axis=1, tiled=True)]
    all_to_all x2 -> x0, starting transfers between devices: 6.68 us -> none  [the longest x1 3.34 us: on_device(): lax.all_to_all(positions, 'col', split_axis=1, concat_axis=1, tiled=True)]
    ppermute x2 -> x0, starting transfers between devices: 3.88 us -> none  [the longest x1 2.25 us: padded_2(): after = lax.ppermute(leading, axis, down)]
    ppermute x2 -> x0, waiting for transfers between devices: 1.95 us -> none  [the longest x1 1.92 us: padded_2(): before = lax.ppermute(last, axis, up)]
    unnamed x1 -> x0, other arithmetic: 1.36 us -> none
  transfers between devices with their start and end apart: 4 -> 0, of which waited for: 3 -> 0; matrix products, arithmetic and copies ran while one was open for 4% -> 0% of each run, Pallas kernels for 0% -> 0%
where the time goes in v1:
time: 27.1 us; the launch traced here: 26.8 us
  Pallas kernels  25.5 us (94%)
  local copies, waits for them, and re-layouts  1.35 us (5%)
    pallas_call x1, Pallas kernels, exchange(): pl.pallas_call(functools.partial(exchange_kernel, rows, cols), out_shape=...  12.9 us
    pallas_call x1, Pallas kernels, forces(): pl.pallas_call(force_kernel, out_shape=jax.ShapeDtypeStruct((3, leaves *...  12.6 us
    unnamed x1, local copies, waits for them, and re-layouts  1.35 us

profile of v1, /device:TPU:0, one launch (start us, length us, event | category | flops | bytes accessed | tf_op | source)
XLA Modules:
  0.0 26.8 jit_solution(9366854685815171657)
XLA Ops:
  0.0 1.4 %copy.5.sources = s32[16,8]{1,0:T(8,128)} copy(s32[16,8]{0,1:T(8,128)} %param.7) | data formatting | bytes 1024 | tf_op args[3]
  1.4 12.9 %exchange.1 = f32[3,8,8,128]{3,2,1,0:T(8,128)} custom-call(f32[3,2048]{1,0:T(4,128)} %pos_hbm.1, f32[1,2048]{1,0:T(1,128)} %mass_hbm.1, s32[1,16]{1,0:T(1,128)} %counts_hbm.1), custom_call_target="tpu_custom_call" | custom-call | tf_op jit(solution)/shard_map/exchange/pallas_call | solution.py:122
  14.2 12.6 %forces.1 = f32[3,2048]{1,0:T(4,128)} custom-call(s32[16,8]{1,0:T(8,128)} %copy.5.sources, f32[192,128]{1,0:T(8,128)} %bitcast.1), custom_call_target="tpu_custom_call" | custom-call | tf_op jit(solution)/shard_map/forces/pallas_call | solution.py:204
